TPU v7x, 32 devices: a whole 2x2x4 slice. The times are simulated.
32 devices in a mesh: replica: 8 (over y, x, core), tok: 4 (over z).
Axes of the slice: x: 2, y: 2, z: 4, core: 2. Of those that a mesh axis runs over, the one named last changes fastest.
Arguments:
- activations: bfloat16 [8192, 2880], P(('replica', 'tok')), may hold values from -6 to 6
- cotangent: bfloat16 [8192, 512], P(('replica', 'tok')), may hold values from -6 to 6
- next_inputs: bfloat16 [8192, 2880], P(('replica', 'tok')), may hold values from -6 to 6
- weight_tiles: bfloat16 [360, 4096], P('tok'), may hold values from -0.109375 to 0.109375
- momentum: float32 [8, 360, 4096], P('replica', 'tok'), may hold values from -6 to 6
- chosen: int32 [8, 4, 8], P('replica', 'tok'), may hold values from 0 to 89, as said below
- counts: int32 [8, 4], P('replica', 'tok'), may hold values from 1 to 8, as said below
Outputs:
- values: bfloat16 [8192, 512], P(('replica', 'tok'))
- new_momentum: float32 [8, 360, 4096], P('replica', 'tok')
Inputs may be any that keep to these rules, and one draw needn't show every extreme that they name: Each list chosen[r, k] names 8 different tile numbers of the shard's 90 tiles; only the first counts[r, k] of them are selected. `counts`: in every draw some token shard has 8 selected tiles in every replica.
All inputs are finite; a program needn't handle non-finite values.
Results may differ from a plain program's by a relative error of at most 0.015.
Values may be sent and summed in bfloat16 or wider, within the bound.
No kernel may reach another device: no remote copies, remote signals or barrier semaphores. Data moves between devices by JAX's collectives and lax.ppermute only.
A program may use at most 64 MiB of HBM per device.

v0:
```python
import math
import jax
import jax.numpy as jnp
from jax import lax
from jax.sharding import PartitionSpec as P

TILE = 64
KEEP = 32
momentum_decay = 0.9
step_size = 0.01


def cosine_rows(count):
    frequency = jnp.arange(count, dtype=jnp.float32)[:, None]
    position = jnp.arange(TILE, dtype=jnp.float32)[None, :]
    cosines = jnp.cos(math.pi * (2.0 * position + 1.0) * frequency / (2.0 * TILE))
    factor = jnp.where(frequency == 0, math.sqrt(1.0 / TILE), math.sqrt(2.0 / TILE))
    return cosines * factor


def rebuild(summed, weight_part, keep_rows):
    quads = summed.reshape(summed.shape[0], KEEP, KEEP)
    update = jnp.einsum(
        "ua,tuv,vb->tab", keep_rows, quads, keep_rows, precision=lax.Precision.HIGHEST
    )
    shifted = weight_part.astype(jnp.float32) - step_size * update.reshape(
        summed.shape[0], TILE * TILE
    )
    return shifted.astype(jnp.bfloat16)


def forward(inputs, new_tiles):
    row_tiles = inputs.shape[1] // TILE
    col_tiles = new_tiles.shape[0] // row_tiles
    blocks = inputs.reshape(inputs.shape[0], row_tiles, TILE)
    matrix = new_tiles.reshape(row_tiles, col_tiles, TILE, TILE)
    output = jnp.einsum("tra,rcab->tcb", blocks, matrix, preferred_element_type=jnp.float32)
    return output.reshape(inputs.shape[0], col_tiles * TILE).astype(jnp.bfloat16)


def local(activations, cotangent, next_inputs, weight_tiles, momentum, chosen, counts):
    highest = lax.Precision.HIGHEST
    shards = lax.axis_size("tok")
    tiles_here = weight_tiles.shape[0]
    row_tiles = activations.shape[1] // TILE
    col_tiles = cotangent.shape[1] // TILE
    grad_scale = 1.0 / math.sqrt(activations.shape[0] * shards)
    keep_rows = cosine_rows(KEEP)
    row_span = min(tiles_here * lax.axis_size("tok") // col_tiles + 2, row_tiles)
    product = (
        lax.dot_general(
            activations, cotangent, (((0,), (0,)), ((), ())), preferred_element_type=jnp.float32
        )
        * grad_scale
    )
    tiled = product.reshape(row_span, TILE, col_tiles, TILE).transpose(0, 2, 1, 3)
    tiled = tiled.reshape(row_span * col_tiles, TILE * TILE)
    gradient = lax.psum_scatter(
        tiled.astype(jnp.bfloat16), "tok", scatter_dimension=0, tiled=True
    ).astype(jnp.float32)
    updated = momentum_decay * momentum[0] + gradient
    chosen_here = chosen[0, 0]
    in_list = jnp.arange(chosen_here.shape[0], dtype=jnp.int32) < counts[0, 0]
    picked = jnp.take(updated, chosen_here, axis=0).reshape(-1, TILE, TILE)
    quadrant = jnp.einsum("ua,nab,vb->nuv", keep_rows, picked, keep_rows, precision=highest)
    quadrant = jnp.where(in_list[:, None, None], quadrant, 0.0).astype(jnp.bfloat16)
    rebuilt = jnp.einsum(
        "ua,nuv,vb->nab", keep_rows, quadrant.astype(jnp.float32), keep_rows, precision=highest
    )
    new_momentum = updated.at[chosen_here].add(-rebuilt.reshape(-1, TILE * TILE))
    listed = jnp.where(in_list, chosen_here, -1)
    flat_quads = quadrant.reshape(-1, KEEP * KEEP)
    tile_numbers = jnp.arange(tiles_here, dtype=jnp.int32)
    all_quads, all_listed = (
        lax.all_gather(flat_quads, "replica", axis=0, tiled=True),
        lax.all_gather(listed, "replica", axis=0, tiled=True),
    )
    one_hot = (all_listed[:, None] == tile_numbers[None, :]).astype(jnp.bfloat16)
    summed = lax.dot_general(
        one_hot, all_quads, (((0,), (0,)), ((), ())), preferred_element_type=jnp.float32
    )
    new_part = rebuild(summed, weight_tiles, keep_rows)
    new_full = lax.all_gather(new_part, "tok", axis=0, tiled=True)
    values = forward(next_inputs, new_full)
    return (values, new_momentum[None])


def solution(mesh):
    return jax.shard_map(
        local,
        mesh=mesh,
        in_specs=(
            P(("replica", "tok"), None),
            P(("replica", "tok"), None),
            P(("replica", "tok"), None),
            P("tok", None),
            P("replica", "tok", None),
            P("replica", "tok", None),
            P("replica", "tok"),
        ),
        out_specs=(P(("replica", "tok"), None), P("replica", "tok", None)),
        check_vma=False,
    )
```

profile of v0, /device:TPU:0, one launch (start us, length us, event | category | flops | bytes accessed | tf_op | source)
XLA Modules:
  0.0 222.4 jit_solution(13789088672530609271)
XLA Ops:
  7.2 0.0 copy-start
  7.2 0.0 all-gather.3.cloned.1.call-start
  7.2 1.3 copy-done
  8.5 3.5 %multiply_convert_fusion = bf16[2880,512]{1,0:T(8,128)(2,1)} fusion(bf16[256,2880]{0,1:T(8,128)(2,1)S(1)} %copy-done, bf16[256,512]{1,0:T(8,128)(2,1)} %param.8), kind=kOutput, calls=%fused_computation.2 | convolution fusion | flops 757923840 | bytes 4685824 | tf_op jit(solution)/shard_map/dot_general | solution.py:51
  12.1 8.4 %convert_element_type.37 = bf16[45,64,8,64]{3,2,1,0:T(8,128)(2,1)} reshape(bf16[2880,512]{1,0:T(8,128)(2,1)} %multiply_convert_fusion) | data formatting | bytes 5898240 | tf_op jit(solution)/shard_map/convert_element_type | solution.py:59
  20.5 7.0 %copy.22 = bf16[45,8,64,64]{3,2,1,0:T(8,128)(2,1)} copy(bf16[45,8,64,64]{3,1,2,0:T(8,128)(2,1)} %bitcast.59) | data formatting | bytes 5898240 | tf_op jit(solution)/shard_map/convert_element_type | solution.py:59
  27.5 8.7 %convert_element_type.39 = bf16[360,4096]{1,0:T(8,128)(2,1)} reshape(bf16[45,8,64,64]{3,2,1,0:T(8,128)(2,1)} %copy.22) | data formatting | bytes 5898240 | tf_op jit(solution)/shard_map/convert_element_type | solution.py:59
  36.2 0.0 copy-start.3
  36.2 0.0 copy-start.4
  36.2 0.0 copy-start.2
  36.2 61.9 %fusion = bf16[96,4096]{1,0:T(8,128)(2,1)S(1)} fusion(bf16[360,4096]{1,0:T(8,128)(2,1)} %convert_element_type.39), kind=kCustom, calls=%all-reduce-scatter | all-reduce-scatter fusion | flops 1572865 | bytes 3736064
  98.2 1.7 collective-permute-start
  99.9 0.0 copy-done.3
  100.6 0.0 copy-done.4
  100.6 0.6 dynamic-slice
  101.9 0.1 fusion.39
  102.0 0.0 copy-done.2
  102.0 0.6 dynamic-slice.5
  103.2 8.0 %all-reduce = s32[64]{0:T(128)S(1)} all-reduce(s32[64]{0:T(128)S(1)} %fusion.39), channel_id=1, replica_groups=mesh['replica'=8,'tok'=4] {'replica'}, use_global_device_ids=true, to_apply=%add | all-reduce | flops 64 | bytes 512
  111.2 0.0 collective-permute-done
  111.3 5.8 %concatenate = bf16[114,4096]{1,0:T(8,128)(2,1)} concatenate(bf16[18,4096]{1,0:T(8,128)(2,1)S(1)} %collective-permute-done, bf16[96,4096]{1,0:T(8,128)(2,1)S(1)} %fusion), dimensions={0} | concatenate | bytes 1867776
  117.1 2.9 %bitcast_add_fusion = f32[90,4096]{1,0:T(8,128)S(1)} fusion(f32[1,90,4096]{2,0,1:T(1,128)} %param.11, bf16[114,4096]{1,0:T(8,128)(2,1)} %concatenate, u32[]{:S(6)} %subtract), kind=kLoop, calls=%fused_computation.4 | loop fusion | flops 1105920 | bytes 3686404 | tf_op jit(solution)/shard_map/add | solution.py:61
  119.9 0.6 gather_fusion
  120.5 0.1 gather.7
  120.6 0.4 fusion.7
  121.0 0.3 fusion.2
  121.3 0.1 reshape.90
  121.5 8.7 %all_gather.10 = bf16[64,1024]{1,0:T(8,128)(2,1)S(1)} all-gather(bf16[8,1024]{1,0:T(8,128)(2,1)S(1)} %reshape.90), channel_id=1, replica_groups=mesh['replica'=8,'tok'=4] {'replica'}, dimensions={0}, use_global_device_ids=true | all-gather | bytes 147456 | tf_op jit(solution)/shard_map/all_gather | solution.py:75
  130.2 0.3 fusion.11
  130.5 1.4 fusion.5
  131.9 3.9 %convolution_multiply_fusion = f32[90,64,64]{0,2,1:T(8,128)} fusion(f32[90,32,64]{0,2,1:T(8,128)S(1)} %fusion.5, f32[32]{0:T(128)S(1)} %compare_select_fusion.2, f32[64]{0:T(128)S(1)} %add_multiply_fusion), kind=kOutput, calls=%fused_computation.3 | convolution fusion | flops 141932544 | bytes 2212224 | tf_op jit(solution)/shard_map/ua,tuv,vb->tab/dot_general | solution.py:23
  135.8 2.8 %copy.26 = f32[90,4096]{1,0:T(8,128)} copy(f32[90,4096]{0,1:T(8,128)} %bitcast.61) | data formatting | bytes 2949120 | tf_op jit(solution)/shard_map/mul | solution.py:26
  138.6 2.6 %fusion.4 = bf16[1,90,4096]{2,1,0:T(8,128)(2,1)} fusion(f32[90,4096]{1,0:T(8,128)} %copy.26, bf16[90,4096]{1,0:T(8,128)(2,1)} %param.10), kind=kLoop, calls=%fused_computation.13 | loop fusion | flops 1105920 | bytes 2949120
  141.2 0.0 all-gather.3.cloned.1.call-update
  141.3 0.3 fusion.13
  141.6 0.6 convolution_negate_fusion
  142.2 0.1 reshape.106
  142.3 1.3 scatter_fusion
  143.7 2.6 %copy.30 = f32[1,90,4096]{2,0,1:T(1,128)} copy(f32[1,90,4096]{2,1,0:T(8,128)S(1)} %bitcast.60) | data formatting | bytes 2949120
  146.3 0.0 copy-start.1
  146.3 55.8 %all-gather.3.cloned.1.call-done = bf16[4,90,4096]{2,1,0:T(8,128)(2,1)} async-done(((bf16[1,90,4096]{2,1,0:T(8,128)(2,1)}), bf16[4,90,4096]{2,1,0:T(8,128)(2,1)}) %all-gather.3.cloned.1.call-update) | async-done | bytes 2949136 | tf_op jit(solution)/shard_map/all_gather | solution.py:83
  202.1 8.2 %reshape.92 = bf16[45,8,64,64]{3,2,1,0:T(8,128)(2,1)} reshape(bf16[4,90,4096]{2,1,0:T(8,128)(2,1)} %all-gather.3.cloned.1.call-done) | data formatting | bytes 5898240 | tf_op jit(solution)/shard_map/reshape | solution.py:36
  210.2 0.0 copy-done.1
  210.2 4.4 %fusion.1 = bf16[8,64,256]{2,1,0:T(8,128)(2,1)S(1)} fusion(bf16[45,8,64,64]{3,2,1,0:T(8,128)(2,1)} %reshape.92, bf16[256,45,64,1]{0,2,3,1:T(8,128)(2,1)S(1)} %bitcast.63), kind=kOutput, calls=%fused_computation.8 | convolution fusion | flops 755105792 | bytes 4685824 | tf_op jit(solution)/shard_map/tra,rcab->tcb/dot_general | solution.py:37
  214.7 0.8 copy.29
  (8 shorter events, 0.1 us)
Async XLA Ops:
  7.2 1.4 copy-start
  7.2 194.9 %all-gather.3.cloned.1.call-start = ((), (), s32[]{:S(2)}) async-start(), calls=%async_computation | async-start | bytes 3932160 | tf_op jit(solution)/shard_map/all_gather | solution.py:83
  36.2 63.7 %copy-start.3 = (s32[1,1,8]{2,1,0:T(1,128)S(1)}, s32[1,1,8]{2,1,0:T(1,128)}, u32[]{:S(2)}) copy-start(s32[1,1,8]{2,1,0:T(1,128)} %param.12) | copy-start | bytes 100
  36.2 64.4 %copy-start.4 = (u32[32]{0:T(128)S(1)}, u32[32]{0:T(128)}, u32[]{:S(2)}) copy-start(u32[32]{0:T(128)} %constant.48) | copy-start | bytes 388
  36.2 65.8 %copy-start.2 = (u32[32]{0:T(128)S(1)}, u32[32]{0:T(128)}, u32[]{:S(2)}) copy-start(u32[32]{0:T(128)} %constant.54) | copy-start | bytes 388
  98.2 13.1 %collective-permute-start = (bf16[18,4096]{1,0:T(8,128)(2,1)S(1)}, bf16[18,4096]{1,0:T(8,128)(2,1)S(1)}, u32[]{:S(2)}, u32[]{:S(2)}) collective-permute-start(bf16[18,4096]{1,0:T(8,128)(2,1)S(1)} %slice.2), channel_id=1, source_target_pairs={{0,1},{1,2},{2,3},{4,5},{5,6},{6,7},{8,9},{9,10},{10,11},{12,13},{... | collective-permute-start | bytes 442376
  146.3 64.0 %copy-start.1 = (bf16[256,2880]{0,1:T(8,128)(2,1)S(1)}, bf16[256,2880]{0,1:T(8,128)(2,1)}, u32[]{:S(2)}) copy-start(bf16[256,2880]{0,1:T(8,128)(2,1)} %param.9) | copy-start | bytes 4423684
Sparse Core Ops, SparseCore 0:
  141.4 60.6 all-gather.2
where the time goes:
time: 224 us; the launch traced here: 222 us
  blocking collectives  78.7 us (35%)
  waiting for transfers between devices  55.8 us (25%)
  local copies, waits for them, and re-layouts  47.9 us (21%)
  between operations  16.2 us (7%)
  matrix products  15.1 us (7%)
  other arithmetic  6.99 us (3%)
    unnamed x2, blocking collectives  69.9 us
    all_gather x1, waiting for transfers between devices, local(): new_full = lax.all_gather(new_part, 'tok', axis=0, tiled=True)  55.8 us
    convert_element_type x3, local copies, waits for them, and re-layouts, local(): tiled.astype(jnp.bfloat16)  24.1 us
    unnamed x17, local copies, waits for them, and re-layouts  11.9 us
    all_gather x1, blocking collectives, local(): lax.all_gather(flat_quads, 'replica', axis=0, tiled=True)  8.73 us
    reshape x1, local copies, waits for them, and re-layouts, forward(): matrix = new_tiles.reshape(row_tiles, col_tiles, TILE, TILE)  8.17 us
    dot_general x2, matrix products, rebuild(): jnp.einsum('ua,tuv,vb->tab', keep_rows, quads, keep_rows, precision=lax.P...  5.25 us
  transfers between devices with their start and end apart: 2, of which 1 were waited for; matrix products, arithmetic and copies ran while one was open for 3% of the time, Pallas kernels for 0%

commit v1 on v0

--- a/solution.py
+++ b/solution.py
@@ -8,6 +8,12 @@
 KEEP = 32
 momentum_decay = 0.9
 step_size = 0.01
+
+
+def in_order(blocks, dim):
+    blocks = jnp.moveaxis(blocks, 0, dim)
+    dims = blocks.shape
+    return blocks.reshape(*dims[:dim], dims[dim] * dims[dim + 1], *dims[dim + 2 :])
 
 
 def cosine_rows(count):
@@ -80,7 +86,19 @@
         one_hot, all_quads, (((0,), (0,)), ((), ())), preferred_element_type=jnp.float32
     )
     new_part = rebuild(summed, weight_tiles, keep_rows)
-    new_full = lax.all_gather(new_part, "tok", axis=0, tiled=True)
+    count_2 = lax.axis_size("tok")
+    pairs = [(i, (i + 1) % count_2) for i in range(count_2)]
+    back = [(b, a) for a, b in pairs]
+    lower, upper = ([], [])
+    for turn in range(count_2 - 1):
+        if turn % 2 == 0:
+            lower.append(lax.ppermute(lower[-1] if lower else new_part, "tok", pairs))
+        else:
+            upper.append(lax.ppermute(upper[-1] if upper else new_part, "tok", back))
+    tiles = jnp.stack([*lower[::-1], new_part, *upper])
+    shift = lax.axis_index("tok") - len(lower)
+    tiles = tiles[(jnp.arange(count_2) - shift) % count_2]
+    new_full = in_order(tiles, 0)
     values = forward(next_inputs, new_full)
     return (values, new_momentum[None])
 

time: 224 us -> 213 us (0.951)
  between operations: 16.2 us -> 2.77 us
  waiting for transfers between devices: 55.8 us -> 46.8 us
  local copies, waits for them, and re-layouts: 47.9 us -> 52.4 us
  starting transfers between devices: 1.74 us -> 5.53 us
  other arithmetic: 6.99 us -> 10.5 us
    all_gather x1 -> x0, waiting for transfers between devices: 55.8 us -> none  [local(): new_full = lax.all_gather(new_part, 'tok', axis=0, tiled=True)]
    ppermute x0 -> x3, waiting for transfers between devices: none -> 46.8 us  [the longest x2 37.4 us: local(): lower.append(lax.ppermute(lower[-1] if lower else new_part, 'tok', pairs))]
    another operation x0 -> x1, local copies, waits for them, and re-layouts: none -> 8.28 us  [forward(): matrix = new_tiles.reshape(row_tiles, col_tiles, TILE, TILE)]
    reshape x1 -> x0, local copies, waits for them, and re-layouts: 8.17 us -> none  [forward(): matrix = new_tiles.reshape(row_tiles, col_tiles, TILE, TILE)]
    gather x0 -> x1, local copies, waits for them, and re-layouts: none -> 4.35 us  [local(): tiles = tiles[(jnp.arange(count_2) - shift) % count_2]]
    ppermute x0 -> x3, starting transfers between devices: none -> 3.83 us  [the longest x1 3.49 us: local(): upper.append(lax.ppermute(upper[-1] if upper else new_part, 'tok', back))]
    another operation x0 -> x1, other arithmetic: none -> 3.44 us  [local(): tiles = jnp.stack([*lower[::-1], new_part, *upper])]
    convert_element_type x0 -> x1, other arithmetic: none -> 2.65 us  [rebuild(): return shifted.astype(jnp.bfloat16)]
  transfers between devices with their start and end apart: 2 -> 4, of which waited for: 1 -> 3; matrix products, arithmetic and copies ran while one was open for 3% -> 3% of each run, Pallas kernels for 0% -> 0%
where the time goes in v1:
time: 213 us; the launch traced here: 212 us
  blocking collectives  78.5 us (37%)
  local copies, waits for them, and re-layouts  52.4 us (25%)
  waiting for transfers between devices  46.8 us (22%)
  matrix products  15.1 us (7%)
  other arithmetic  10.5 us (5%)
  starting transfers between devices  5.53 us (3%)
  between operations  2.77 us (1%)
    unnamed x2, blocking collectives  69.9 us
    ppermute x2, waiting for transfers between devices, local(): lower.append(lax.ppermute(lower[-1] if lower else new_part, 'tok', pairs))  37.4 us
    convert_element_type x3, local copies, waits for them, and re-layouts, local(): tiled.astype(jnp.bfloat16)  24.1 us
    unnamed x17, local copies, waits for them, and re-layouts  11.9 us
    ppermute x1, waiting for transfers between devices, local(): upper.append(lax.ppermute(upper[-1] if upper else new_part, 'tok', back))  9.37 us
    all_gather x1, blocking collectives, local(): lax.all_gather(flat_quads, 'replica', axis=0, tiled=True)  8.55 us
    another operation x1, local copies, waits for them, and re-layouts, forward(): matrix = new_tiles.reshape(row_tiles, col_tiles, TILE, TILE)  8.28 us
    dot_general x2, matrix products, rebuild(): jnp.einsum('ua,tuv,vb->tab', keep_rows, quads, keep_rows, precision=lax.P...  5.25 us
  transfers between devices with their start and end apart: 4, of which 3 were waited for; matrix products, arithmetic and copies ran while one was open for 3% of the time, Pallas kernels for 0%

profile of v1, /device:TPU:0, one launch (start us, length us, event | category | flops | bytes accessed | tf_op | source)
XLA Modules:
  0.0 211.6 jit_solution(5993817045334967657)
XLA Ops:
  0.6 0.0 copy-start
  0.6 1.4 copy-done
  2.0 3.5 %multiply_convert_fusion = bf16[2880,512]{1,0:T(8,128)(2,1)} fusion(bf16[256,2880]{0,1:T(8,128)(2,1)S(1)} %copy-done, bf16[256,512]{1,0:T(8,128)(2,1)} %param.8), kind=kOutput, calls=%fused_computation.3 | convolution fusion | flops 757923840 | bytes 4685824 | tf_op jit(solution)/shard_map/dot_general | solution.py:57
  5.5 8.4 %convert_element_type.37 = bf16[45,64,8,64]{3,2,1,0:T(8,128)(2,1)} reshape(bf16[2880,512]{1,0:T(8,128)(2,1)} %multiply_convert_fusion) | data formatting | bytes 5898240 | tf_op jit(solution)/shard_map/convert_element_type | solution.py:65
  13.9 7.0 %copy.23 = bf16[45,8,64,64]{3,2,1,0:T(8,128)(2,1)} copy(bf16[45,8,64,64]{3,1,2,0:T(8,128)(2,1)} %bitcast.63) | data formatting | bytes 5898240 | tf_op jit(solution)/shard_map/convert_element_type | solution.py:65
  20.9 8.7 %convert_element_type.39 = bf16[360,4096]{1,0:T(8,128)(2,1)} reshape(bf16[45,8,64,64]{3,2,1,0:T(8,128)(2,1)} %copy.23) | data formatting | bytes 5898240 | tf_op jit(solution)/shard_map/convert_element_type | solution.py:65
  29.7 0.0 copy-start.3
  29.7 0.0 copy-start.4
  29.7 61.9 %fusion = bf16[96,4096]{1,0:T(8,128)(2,1)S(1)} fusion(bf16[360,4096]{1,0:T(8,128)(2,1)} %convert_element_type.39), kind=kCustom, calls=%all-reduce-scatter | all-reduce-scatter fusion | flops 1572865 | bytes 3736064
  91.6 1.7 collective-permute-start.3
  93.4 0.0 copy-done.3
  94.1 0.0 copy-done.4
  94.1 0.6 dynamic-slice
  95.3 0.1 fusion.40
  95.4 0.0 copy-done.2
  95.4 0.6 dynamic-slice.5
  96.7 8.0 %all-reduce = s32[64]{0:T(128)S(1)} all-reduce(s32[64]{0:T(128)S(1)} %fusion.40), channel_id=1, replica_groups=mesh['replica'=8,'tok'=4] {'replica'}, use_global_device_ids=true, to_apply=%add | all-reduce | flops 64 | bytes 512
  104.7 0.0 collective-permute-done.3
  104.7 5.8 %concatenate = bf16[114,4096]{1,0:T(8,128)(2,1)} concatenate(bf16[18,4096]{1,0:T(8,128)(2,1)S(1)} %collective-permute-done.3, bf16[96,4096]{1,0:T(8,128)(2,1)S(1)} %fusion), dimensions={0} | concatenate | bytes 1867776
  110.5 2.9 %bitcast_add_fusion = f32[90,4096]{1,0:T(8,128)S(1)} fusion(f32[1,90,4096]{2,0,1:T(1,128)} %param.11, bf16[114,4096]{1,0:T(8,128)(2,1)} %concatenate, u32[]{:S(6)} %subtract), kind=kLoop, calls=%fused_computation.6 | loop fusion | flops 1105920 | bytes 3686404 | tf_op jit(solution)/shard_map/add | solution.py:67
  113.4 0.6 gather_fusion
  114.0 0.1 gather.10
  114.1 0.4 fusion.6
  114.5 0.3 fusion.2
  114.8 0.1 reshape.136
  114.9 8.5 %all_gather.7 = bf16[64,1024]{1,0:T(8,128)(2,1)S(1)} all-gather(bf16[8,1024]{1,0:T(8,128)(2,1)S(1)} %reshape.136), channel_id=1, replica_groups=mesh['replica'=8,'tok'=4] {'replica'}, dimensions={0}, use_global_device_ids=true | all-gather | bytes 147456 | tf_op jit(solution)/shard_map/all_gather | solution.py:81
  123.5 0.3 fusion.10
  123.8 1.4 fusion.4
  125.2 3.9 %convolution_multiply_fusion = f32[90,64,64]{0,2,1:T(8,128)} fusion(f32[90,32,64]{0,2,1:T(8,128)S(1)} %fusion.4, f32[32]{0:T(128)S(1)} %compare_select_fusion.5, f32[64]{0:T(128)S(1)} %add_multiply_fusion), kind=kOutput, calls=%fused_computation.5 | convolution fusion | flops 141932544 | bytes 2212224 | tf_op jit(solution)/shard_map/ua,tuv,vb->tab/dot_general | solution.py:29
  129.0 2.8 %copy.27 = f32[90,4096]{1,0:T(8,128)} copy(f32[90,4096]{0,1:T(8,128)} %bitcast.65) | data formatting | bytes 2949120 | tf_op jit(solution)/shard_map/mul | solution.py:32
  131.9 2.7 %subtract_convert_fusion = bf16[90,4096]{1,0:T(8,128)(2,1)} fusion(f32[90,4096]{1,0:T(8,128)} %copy.27, bf16[90,4096]{1,0:T(8,128)(2,1)} %param.10), kind=kLoop, calls=%fused_computation.8 | loop fusion | flops 1105920 | bytes 2949120 | tf_op jit(solution)/shard_map/convert_element_type | solution.py:35
  134.5 0.3 collective-permute-start
  134.9 3.5 %collective-permute-start.2 = (bf16[90,4096]{1,0:T(8,128)(2,1)}, bf16[90,4096]{1,0:T(8,128)(2,1)}, u32[]{:S(2)}, u32[]{:S(2)}) collective-permute-start(bf16[90,4096]{1,0:T(8,128)(2,1)} %subtract_convert_fusion), channel_id=1, source_target_pairs={{1,0},{2,1},{3,2},{0,3},{5,4},{6,5},{7,6},{4,7},{9,8},{10,9},{11,1... | collective-permute-start | bytes 2211848 | tf_op jit(solution)/shard_map/ppermute | solution.py:97
  138.4 18.8 %collective-permute-done = bf16[90,4096]{1,0:T(8,128)(2,1)} collective-permute-done((bf16[90,4096]{1,0:T(8,128)(2,1)}, bf16[90,4096]{1,0:T(8,128)(2,1)}, u32[]{:S(2)}, u32[]{:S(2)}) %collective-permute-start) | collective-permute-done | bytes 737312 | tf_op jit(solution)/shard_map/ppermute | solution.py:95
  157.1 0.0 collective-permute-start.1
  157.1 0.3 fusion.12
  157.4 0.6 convolution_negate_fusion
  158.1 0.1 reshape.159
  158.2 1.3 scatter_fusion
  159.6 2.6 %copy.31 = f32[1,90,4096]{2,0,1:T(1,128)} copy(f32[1,90,4096]{2,1,0:T(8,128)S(1)} %bitcast.64) | data formatting | bytes 2949120
  162.2 9.4 %collective-permute-done.2 = bf16[90,4096]{1,0:T(8,128)(2,1)} collective-permute-done((bf16[90,4096]{1,0:T(8,128)(2,1)}, bf16[90,4096]{1,0:T(8,128)(2,1)}, u32[]{:S(2)}, u32[]{:S(2)}) %collective-permute-start.2) | collective-permute-done | bytes 737312 | tf_op jit(solution)/shard_map/ppermute | solution.py:97
  171.6 18.6 %collective-permute-done.1 = bf16[90,4096]{1,0:T(8,128)(2,1)} collective-permute-done((bf16[90,4096]{1,0:T(8,128)(2,1)}, bf16[90,4096]{1,0:T(8,128)(2,1)}, u32[]{:S(2)}, u32[]{:S(2)}) %collective-permute-start.1) | collective-permute-done | bytes 737312 | tf_op jit(solution)/shard_map/ppermute | solution.py:95
  190.2 3.4 %pad_maximum_fusion = bf16[4,90,4096]{2,1,0:T(8,128)(2,1)} fusion(bf16[1,90,4096]{2,1,0:T(8,128)(2,1)} %bitcast.13, bf16[1,90,4096]{2,1,0:T(8,128)(2,1)} %bitcast.12, bf16[1,90,4096]{2,1,0:T(8,128)(2,1)} %bitcast.11, bf16[1,90,4096]{2,1,0:T(8,128)(2,1)} %bitcast.10), kind=kLoop, calls=%fused_computation.4 | loop fusion | flops 4423680 | bytes 5898240 | tf_op jit(solution)/shard_map/stack | solution.py:98
  193.6 4.3 %gather_fusion.1 = bf16[4,90,4096]{2,1,0:T(8,128)(2,1)} fusion(bf16[4,90,4096]{2,1,0:T(8,128)(2,1)} %pad_maximum_fusion, s32[1024]{0:T(1024)S(1)} %pad_clamp_fusion), kind=kCustom, calls=%fused_computation.1 | custom fusion | bytes 5898256 | tf_op jit(solution)/shard_map/gather | solution.py:100
  198.0 8.3 %reshape_reshape.3 = bf16[45,8,64,64]{3,2,1,0:T(8,128)(2,1)} reshape(bf16[4,90,4096]{2,1,0:T(8,128)(2,1)} %gather_fusion.1) | data formatting | bytes 5898240 | tf_op jit(solution)/shard_map/reshape;reshape | solution.py:42
  206.3 0.0 copy-done.1
  206.3 4.4 %fusion.1 = bf16[8,64,256]{2,1,0:T(8,128)(2,1)S(1)} fusion(bf16[45,8,64,64]{3,2,1,0:T(8,128)(2,1)} %reshape_reshape.3, bf16[256,45,64,1]{0,2,3,1:T(8,128)(2,1)S(1)} %bitcast.67), kind=kOutput, calls=%fused_computation.10 | convolution fusion | flops 755105792 | bytes 4685824 | tf_op jit(solution)/shard_map/tra,rcab->tcb/dot_general | solution.py:43
  210.7 0.8 copy.30
  (12 shorter events, 0.1 us)
Async XLA Ops:
  0.6 1.4 copy-start
  29.7 63.7 %copy-start.3 = (s32[1,1,8]{2,1,0:T(1,128)S(1)}, s32[1,1,8]{2,1,0:T(1,128)}, u32[]{:S(2)}) copy-start(s32[1,1,8]{2,1,0:T(1,128)} %param.12) | copy-start | bytes 100
  29.7 64.4 %copy-start.4 = (u32[32]{0:T(128)S(1)}, u32[32]{0:T(128)}, u32[]{:S(2)}) copy-start(u32[32]{0:T(128)} %constant.71) | copy-start | bytes 388
  29.7 65.8 %copy-start.2 = (u32[32]{0:T(128)S(1)}, u32[32]{0:T(128)}, u32[]{:S(2)}) copy-start(u32[32]{0:T(128)} %constant.77) | copy-start | bytes 388
  91.6 13.1 %collective-permute-start.3 = (bf16[18,4096]{1,0:T(8,128)(2,1)S(1)}, bf16[18,4096]{1,0:T(8,128)(2,1)S(1)}, u32[]{:S(2)}, u32[]{:S(2)}) collective-permute-start(bf16[18,4096]{1,0:T(8,128)(2,1)S(1)} %slice.4), channel_id=1, source_target_pairs={{0,1},{1,2},{2,3},{4,5},{5,6},{6,7},{8,9},{9,10},{10,11},{12,13},{... | collective-permute-start | bytes 442376
  134.5 22.6 %collective-permute-start = (bf16[90,4096]{1,0:T(8,128)(2,1)}, bf16[90,4096]{1,0:T(8,128)(2,1)}, u32[]{:S(2)}, u32[]{:S(2)}) collective-permute-start(bf16[90,4096]{1,0:T(8,128)(2,1)} %subtract_convert_fusion), channel_id=1, source_target_pairs={{0,1},{1,2},{2,3},{3,0},{4,5},{5,6},{6,7},{7,4},{8,9},{9,10},{10,1... | collective-permute-start | bytes 2211848 | tf_op jit(solution)/shard_map/ppermute | solution.py:95
  134.9 36.7 %collective-permute-start.2 = (bf16[90,4096]{1,0:T(8,128)(2,1)}, bf16[90,4096]{1,0:T(8,128)(2,1)}, u32[]{:S(2)}, u32[]{:S(2)}) collective-permute-start(bf16[90,4096]{1,0:T(8,128)(2,1)} %subtract_convert_fusion), channel_id=1, source_target_pairs={{1,0},{2,1},{3,2},{0,3},{5,4},{6,5},{7,6},{4,7},{9,8},{10,9},{11,1... | collective-permute-start | bytes 2211848 | tf_op jit(solution)/shard_map/ppermute | solution.py:97
  157.1 33.1 %collective-permute-start.1 = (bf16[90,4096]{1,0:T(8,128)(2,1)}, bf16[90,4096]{1,0:T(8,128)(2,1)}, u32[]{:S(2)}, u32[]{:S(2)}) collective-permute-start(bf16[90,4096]{1,0:T(8,128)(2,1)} %collective-permute-done), channel_id=1, source_target_pairs={{0,1},{1,2},{2,3},{3,0},{4,5},{5,6},{6,7},{7,4},{8,9},{9,10},{10,1... | collective-permute-start | bytes 2211848 | tf_op jit(solution)/shard_map/ppermute | solution.py:95
  198.0 8.3 %copy-start.1 = (bf16[256,2880]{0,1:T(8,128)(2,1)S(1)}, bf16[256,2880]{0,1:T(8,128)(2,1)}, u32[]{:S(2)}) copy-start(bf16[256,2880]{0,1:T(8,128)(2,1)} %param.9) | copy-start | bytes 4423684
